TPU v7x, 32 devices: a whole 2x2x4 slice. The times are simulated.
32 devices in a mesh: grp: 4 (over y, x), dev: 8 (over z, core).
Axes of the slice: x: 2, y: 2, z: 4, core: 2. Of those that a mesh axis runs over, the one named last changes fastest.
Arguments:
- particles: float32 [128, 5, 128], P(('grp', 'dev')), as said below
- entropy: float32 [128, 128], P(('grp', 'dev')), may hold values from 0.5 to 2
- lists: int32 [128, 64], P(('grp', 'dev')), may hold values from 0 to 127, as said below
- counts: int32 [128], P(('grp', 'dev')), may hold values from 16 to 64, as said below
Outputs:
- density: float32 [128, 128], P(('grp', 'dev'))
- accel: float32 [128, 3, 128], P(('grp', 'dev'))
Inputs may be any that keep to these rules, and one draw needn't show every extreme that they name: lists[c, 0] = c; every id lies in the group of c or in one of the two groups next to it, counting groups of 32 cells around a loop. `counts`: each count is a multiple of 16. `particles`: coordinates in 0 to 1 within the group's slab, masses positive, smoothing lengths from 0.3 to 0.6.
All inputs are finite; a program needn't handle non-finite values.
Results may differ from a plain program's by a relative error of at most 0.0003.
Values sent between devices are 32-bit elements; how exact they have to be, the bound alone decides.
No kernel may reach another device: no remote copies, remote signals or barrier semaphores. Data moves between devices by JAX's collectives and lax.ppermute only.
A program may use at most 64 MiB of HBM per device.

v0:
```python
import math

import jax
import jax.numpy as jnp
from jax import lax
from jax.sharding import PartitionSpec as P

NB = 64
NBLK = 8


norm_const = 21.0 / (16.0 * math.pi)


def padded(block, sides, width):
    for axis, dim in sides:
        count = lax.axis_size(axis)
        forward = [(i, i + 1) for i in range(count - 1)]
        forward.append((count - 1, 0))
        backward = [(target, source) for source, target in forward]
        low = lax.ppermute(
            lax.slice_in_dim(block, block.shape[dim] - width, None, axis=dim), axis, forward
        )
        high = lax.ppermute(lax.slice_in_dim(block, 0, width, axis=dim), axis, backward)
        block = jnp.concatenate([low, block, high], axis=dim)
    return block


def kernel_parts(dist_sq, smooth):
    ratio = jnp.sqrt(dist_sq) / smooth
    base_of = jnp.maximum(1.0 - 0.5 * ratio, 0.0)
    kernel = norm_const / smooth**3 * base_of**4 * (1.0 + 2.0 * ratio)
    slope = -5.0 * norm_const / smooth**5 * base_of**3
    return (kernel, slope)


def on_device(particles, entropy, lists, counts):
    own_cells = particles.shape[0]
    groups = lax.axis_size("grp")
    members = lax.axis_size("dev")
    group_cells = own_cells * members
    group_at = lax.axis_index("grp")
    group_of = lists // group_cells
    within = lists % group_cells
    side_of = (group_of - group_at + 1 + groups) % groups
    shift_all = (side_of - 1).astype(jnp.float32)
    member_of = within // own_cells
    cell_of = within % own_cells
    rimmed = padded(particles, (("grp", 0),), own_cells)
    extended = lax.all_gather(rimmed, "dev", axis=0, tiled=True)
    slots_ext = member_of * (3 * own_cells) + side_of * own_cells + cell_of
    upper = NB // NBLK
    slot_range = jnp.arange(NBLK, dtype=jnp.int32)
    own_smooth = particles[:, None, 4, :, None]
    unit_first = jnp.array([1.0, 0.0, 0.0], dtype=jnp.float32)

    def fetch_block(block_at):
        chosen = lax.dynamic_slice_in_dim(slots_ext, block_at * NBLK, NBLK, 1)
        shift_blk = lax.dynamic_slice_in_dim(shift_all, block_at * NBLK, NBLK, 1)
        others = extended[chosen]
        live = ((block_at * NBLK + slot_range)[None, :] < counts[:, None]).astype(jnp.float32)
        offset = particles[:, None, :3, :, None] - others[:, :, :3, None, :]
        offset = offset - shift_blk[:, :, None, None, None] * unit_first[None, None, :, None, None]
        dist_sq = jnp.sum(offset * offset, axis=2)
        return (chosen, others, live, offset, dist_sq)

    def density_step(block_at, total):
        chosen, others, live, offset, dist_sq = fetch_block(block_at)
        kernel, slope = kernel_parts(dist_sq, own_smooth)
        return total + jnp.sum(
            live[:, :, None, None] * others[:, :, 3, None, :] * kernel, axis=(1, 3)
        )

    density = lax.fori_loop(
        0, upper, density_step, jnp.zeros((own_cells, particles.shape[2]), jnp.float32)
    )
    pressure = entropy * density ** (5.0 / 3.0)
    weight = pressure / (density * density)
    weight_rim = padded(weight, (("grp", 0),), own_cells)
    weight_ext = lax.all_gather(weight_rim, "dev", axis=0, tiled=True)

    def force_step(block_at, total):
        chosen, others, live, offset, dist_sq = fetch_block(block_at)
        kernel_i, slope_i = kernel_parts(dist_sq, own_smooth)
        kernel_j, slope_j = kernel_parts(dist_sq, others[:, :, 4, None, :])
        factor = (
            live[:, :, None, None]
            * others[:, :, 3, None, :]
            * (weight[:, None, :, None] * slope_i + weight_ext[chosen][:, :, None, :] * slope_j)
        )
        return total - jnp.sum(factor[:, :, None] * offset, axis=(1, 4))

    accel = lax.fori_loop(
        0, upper, force_step, jnp.zeros((own_cells, 3, particles.shape[2]), jnp.float32)
    )
    return (density, accel)


def solution(mesh):
    return jax.shard_map(
        on_device,
        mesh=mesh,
        in_specs=(
            P(("grp", "dev"), None, None),
            P(("grp", "dev"), None),
            P(("grp", "dev"), None),
            P(("grp", "dev")),
        ),
        out_specs=(P(("grp", "dev"), None), P(("grp", "dev"), None, None)),
        check_vma=False,
    )
```

profile of v0, /device:TPU:0, one launch (start us, length us, event | category | flops | bytes accessed | tf_op | source)
XLA Modules:
  0.0 148.0 jit_solution(8237750292582553730)
XLA Ops:
  1.3 3.9 %collective-permute-start.1 = (f32[4,5,128]{2,1,0:T(8,128)S(1)}, f32[4,5,128]{2,1,0:T(8,128)S(1)}, u32[]{:S(2)}, u32[]{:S(2)}) collective-permute-start(f32[4,5,128]{2,1,0:T(8,128)S(1)} %copy.28), channel_id=1, source_target_pairs={{8,0},{16,8},{24,16},{0,24},{9,1},{17,9},{25,17},{1,25},{10,2},{18... | collective-permute-start | bytes 30728 | tf_op jit(solution)/shard_map/ppermute | solution.py:24
  8.0 1.9 %collective-permute-done = f32[4,5,128]{2,1,0:T(8,128)S(1)} collective-permute-done((f32[4,5,128]{2,1,0:T(8,128)S(1)}, f32[4,5,128]{2,1,0:T(8,128)S(1)}, u32[]{:S(2)}, u32[]{:S(2)}) %collective-permute-start) | collective-permute-done | bytes 10272 | tf_op jit(solution)/shard_map/ppermute | solution.py:21
  9.9 14.7 %all_gather.6 = f32[96,5,128]{2,1,0:T(8,128)S(1)} all-gather(f32[12,5,128]{2,1,0:T(8,128)S(1)} %pad_maximum_fusion), channel_id=1, replica_groups=mesh['grp'=4,'dev'=8] {'dev'}, dimensions={0}, use_global_device_ids=true | all-gather | bytes 276480 | tf_op jit(solution)/shard_map/all_gather | solution.py:50
  24.6 41.9 %while.34 = (s32[]{:T(128)}, f32[4,128]{1,0:T(4,128)S(1)}, s32[4]{0:T(128)}, s32[4,64]{1,0:T(4,128)S(1)}, f32[96,5,128]{2,1,0:T(8,128)S(1)}, /*index=5*/f32[4,1,...) while((s32[]{:T(128)}, f32[4,128]{1,0:T(4,128)S(1)}, ...), condition=%wide.region_3.4_spmd.clone.clone, body=%wide.region_0.3_spmd.sunk.clone.clone.sunk | while | flops 12065039 | bytes 4628909 | solution.py:74
  28.4 1.4 multiply_reduce_fusion.9
  33.7 1.4 multiply_reduce_fusion.9
  38.9 1.4 multiply_reduce_fusion.9
  44.1 1.4 multiply_reduce_fusion.9
  49.4 1.4 multiply_reduce_fusion.9
  54.6 1.4 multiply_reduce_fusion.9
  59.9 1.4 multiply_reduce_fusion.9
  65.1 1.4 multiply_reduce_fusion.9
  68.7 1.6 %collective-permute-done.3 = f32[4,128]{1,0:T(4,128)S(1)} collective-permute-done((f32[4,128]{1,0:T(4,128)S(1)}, f32[4,128]{1,0:T(4,128)S(1)}, u32[]{:S(2)}, u32[]{:S(2)}) %collective-permute-start.3) | collective-permute-done | bytes 2080 | tf_op jit(solution)/shard_map/ppermute | solution.py:24
  70.2 2.0 %collective-permute-done.2 = f32[4,128]{1,0:T(4,128)S(1)} collective-permute-done((f32[4,128]{1,0:T(4,128)S(1)}, f32[4,128]{1,0:T(4,128)S(1)}, u32[]{:S(2)}, u32[]{:S(2)}) %collective-permute-start.2) | collective-permute-done | bytes 2080 | tf_op jit(solution)/shard_map/ppermute | solution.py:21
  72.2 14.0 %all-gather = f32[8,12,128]{2,1,0:T(8,128)S(1)} all-gather(f32[1,12,128]{2,1,0:T(8,128)S(1)} %maximum_bitcast_fusion), channel_id=1, replica_groups=mesh['grp'=4,'dev'=8] {'dev'}, dimensions={0}, use_global_device_ids=true | all-gather | bytes 55296 | tf_op jit(solution)/shard_map/all_gather | solution.py:80
  86.2 61.1 %while.35 = (s32[]{:T(128)}, f32[4,3,128]{2,1,0:T(4,128)S(1)}, s32[4]{0:T(128)}, s32[4,64]{1,0:T(4,128)S(1)}, f32[96,5,128]{2,1,0:T(8,128)S(1)}, /*index=5*/f32[...) while((s32[]{:T(128)}, f32[4,3,128]{2,1,0:T(4,128)S(1)}, ...), condition=%wide.region_7.8_spmd.clone.clone, body=%wide.region_4.7_spmd.sunk.clone.clone.sunk | while | flops 21519628 | bytes 9044925 | solution.py:93
  90.6 1.9 %fusion.24 = f32[4,8,128,128]{3,2,1,0:T(8,128)S(1)} fusion(f32[4,8,128,128]{3,2,1,0:T(8,128)S(1)} %multiply_reduce_fusion.10, f32[4,8,128]{2,1,0:T(8,128)S(1)} %bitcast.59, f32[4,8,128]{2,1,0:T(8,128)S(1)} %get-tuple-element.869, f32[4,8,128]{2,1,0:T(8,128)S(1)} %bitcast.60, f32[4,128]{1,0:T(4,128)S(1)} %bitcast.64, ...), kind=kLoop, calls=%fused_computation.25.clone.1 | loop fusion | flops 9437184 | bytes 4265984 | tf_op jit(solution)/shard_map/while/body/eval_jaxpr/mul | solution.py:87
  98.2 1.9 %fusion.24 = f32[4,8,128,128]{3,2,1,0:T(8,128)S(1)} fusion(f32[4,8,128,128]{3,2,1,0:T(8,128)S(1)} %multiply_reduce_fusion.10, f32[4,8,128]{2,1,0:T(8,128)S(1)} %bitcast.59, f32[4,8,128]{2,1,0:T(8,128)S(1)} %get-tuple-element.869, f32[4,8,128]{2,1,0:T(8,128)S(1)} %bitcast.60, f32[4,128]{1,0:T(4,128)S(1)} %bitcast.64, ...), kind=kLoop, calls=%fused_computation.25.clone.1 | loop fusion | flops 9437184 | bytes 4265984 | tf_op jit(solution)/shard_map/while/body/eval_jaxpr/mul | solution.py:87
  105.9 1.9 %fusion.24 = f32[4,8,128,128]{3,2,1,0:T(8,128)S(1)} fusion(f32[4,8,128,128]{3,2,1,0:T(8,128)S(1)} %multiply_reduce_fusion.10, f32[4,8,128]{2,1,0:T(8,128)S(1)} %bitcast.59, f32[4,8,128]{2,1,0:T(8,128)S(1)} %get-tuple-element.869, f32[4,8,128]{2,1,0:T(8,128)S(1)} %bitcast.60, f32[4,128]{1,0:T(4,128)S(1)} %bitcast.64, ...), kind=kLoop, calls=%fused_computation.25.clone.1 | loop fusion | flops 9437184 | bytes 4265984 | tf_op jit(solution)/shard_map/while/body/eval_jaxpr/mul | solution.py:87
  113.5 1.9 %fusion.24 = f32[4,8,128,128]{3,2,1,0:T(8,128)S(1)} fusion(f32[4,8,128,128]{3,2,1,0:T(8,128)S(1)} %multiply_reduce_fusion.10, f32[4,8,128]{2,1,0:T(8,128)S(1)} %bitcast.59, f32[4,8,128]{2,1,0:T(8,128)S(1)} %get-tuple-element.869, f32[4,8,128]{2,1,0:T(8,128)S(1)} %bitcast.60, f32[4,128]{1,0:T(4,128)S(1)} %bitcast.64, ...), kind=kLoop, calls=%fused_computation.25.clone.1 | loop fusion | flops 9437184 | bytes 4265984 | tf_op jit(solution)/shard_map/while/body/eval_jaxpr/mul | solution.py:87
  121.2 1.9 %fusion.24 = f32[4,8,128,128]{3,2,1,0:T(8,128)S(1)} fusion(f32[4,8,128,128]{3,2,1,0:T(8,128)S(1)} %multiply_reduce_fusion.10, f32[4,8,128]{2,1,0:T(8,128)S(1)} %bitcast.59, f32[4,8,128]{2,1,0:T(8,128)S(1)} %get-tuple-element.869, f32[4,8,128]{2,1,0:T(8,128)S(1)} %bitcast.60, f32[4,128]{1,0:T(4,128)S(1)} %bitcast.64, ...), kind=kLoop, calls=%fused_computation.25.clone.1 | loop fusion | flops 9437184 | bytes 4265984 | tf_op jit(solution)/shard_map/while/body/eval_jaxpr/mul | solution.py:87
  128.8 1.9 %fusion.24 = f32[4,8,128,128]{3,2,1,0:T(8,128)S(1)} fusion(f32[4,8,128,128]{3,2,1,0:T(8,128)S(1)} %multiply_reduce_fusion.10, f32[4,8,128]{2,1,0:T(8,128)S(1)} %bitcast.59, f32[4,8,128]{2,1,0:T(8,128)S(1)} %get-tuple-element.869, f32[4,8,128]{2,1,0:T(8,128)S(1)} %bitcast.60, f32[4,128]{1,0:T(4,128)S(1)} %bitcast.64, ...), kind=kLoop, calls=%fused_computation.25.clone.1 | loop fusion | flops 9437184 | bytes 4265984 | tf_op jit(solution)/shard_map/while/body/eval_jaxpr/mul | solution.py:87
  136.4 1.9 %fusion.24 = f32[4,8,128,128]{3,2,1,0:T(8,128)S(1)} fusion(f32[4,8,128,128]{3,2,1,0:T(8,128)S(1)} %multiply_reduce_fusion.10, f32[4,8,128]{2,1,0:T(8,128)S(1)} %bitcast.59, f32[4,8,128]{2,1,0:T(8,128)S(1)} %get-tuple-element.869, f32[4,8,128]{2,1,0:T(8,128)S(1)} %bitcast.60, f32[4,128]{1,0:T(4,128)S(1)} %bitcast.64, ...), kind=kLoop, calls=%fused_computation.25.clone.1 | loop fusion | flops 9437184 | bytes 4265984 | tf_op jit(solution)/shard_map/while/body/eval_jaxpr/mul | solution.py:87
  144.1 1.9 %fusion.24 = f32[4,8,128,128]{3,2,1,0:T(8,128)S(1)} fusion(f32[4,8,128,128]{3,2,1,0:T(8,128)S(1)} %multiply_reduce_fusion.10, f32[4,8,128]{2,1,0:T(8,128)S(1)} %bitcast.59, f32[4,8,128]{2,1,0:T(8,128)S(1)} %get-tuple-element.869, f32[4,8,128]{2,1,0:T(8,128)S(1)} %bitcast.60, f32[4,128]{1,0:T(4,128)S(1)} %bitcast.64, ...), kind=kLoop, calls=%fused_computation.25.clone.1 | loop fusion | flops 9437184 | bytes 4265984 | tf_op jit(solution)/shard_map/while/body/eval_jaxpr/mul | solution.py:87
  (276 shorter events, 81.6 us)
Async XLA Ops:
  1.3 6.7 %collective-permute-start.1 = (f32[4,5,128]{2,1,0:T(8,128)S(1)}, f32[4,5,128]{2,1,0:T(8,128)S(1)}, u32[]{:S(2)}, u32[]{:S(2)}) collective-permute-start(f32[4,5,128]{2,1,0:T(8,128)S(1)} %copy.28), channel_id=1, source_target_pairs={{8,0},{16,8},{24,16},{0,24},{9,1},{17,9},{25,17},{1,25},{10,2},{18... | collective-permute-start | bytes 30728 | tf_op jit(solution)/shard_map/ppermute | solution.py:24
  5.3 4.6 %collective-permute-start = (f32[4,5,128]{2,1,0:T(8,128)S(1)}, f32[4,5,128]{2,1,0:T(8,128)S(1)}, u32[]{:S(2)}, u32[]{:S(2)}) collective-permute-start(f32[4,5,128]{2,1,0:T(8,128)S(1)} %copy.28), channel_id=1, source_target_pairs={{0,8},{8,16},{16,24},{24,0},{1,9},{9,17},{17,25},{25,1},{2,10},{10... | collective-permute-start | bytes 30728 | tf_op jit(solution)/shard_map/ppermute | solution.py:21
  24.6 41.9 %copy-start.1 = (f32[4,128]{1,0:T(4,128)S(1)}, f32[4,128]{1,0:T(4,128)}, u32[]{:S(2)}) copy-start(f32[4,128]{1,0:T(4,128)} %param.10) | copy-start | bytes 6148
  66.6 19.7 %copy-start = (f32[4,128]{1,0:T(4,128)}, f32[4,128]{1,0:T(4,128)S(1)}, u32[]{:S(2)}) copy-start(f32[4,128]{1,0:T(4,128)S(1)} %get-tuple-element.691) | copy-start | bytes 6148
  66.6 3.6 %collective-permute-start.3 = (f32[4,128]{1,0:T(4,128)S(1)}, f32[4,128]{1,0:T(4,128)S(1)}, u32[]{:S(2)}, u32[]{:S(2)}) collective-permute-start(f32[4,128]{1,0:T(4,128)S(1)} %multiply_divide_fusion), channel_id=1, source_target_pairs={{8,0},{16,8},{24,16},{0,24},{9,1},{17,9},{25,17},{1,25},{10,2},{18... | collective-permute-start | bytes 6152 | tf_op jit(solution)/shard_map/ppermute | solution.py:24
  67.7 4.5 %collective-permute-start.2 = (f32[4,128]{1,0:T(4,128)S(1)}, f32[4,128]{1,0:T(4,128)S(1)}, u32[]{:S(2)}, u32[]{:S(2)}) collective-permute-start(f32[4,128]{1,0:T(4,128)S(1)} %multiply_divide_fusion), channel_id=1, source_target_pairs={{0,8},{8,16},{16,24},{24,0},{1,9},{9,17},{17,25},{25,1},{2,10},{10... | collective-permute-start | bytes 6152 | tf_op jit(solution)/shard_map/ppermute | solution.py:21
where the time goes:
time: 149 us; the launch traced here: 148 us
  other arithmetic  86.7 us (58%)
  blocking collectives  28.7 us (19%)
  local copies, waits for them, and re-layouts  19.1 us (13%)
  starting transfers between devices  6 us (4%)
  waiting for transfers between devices  5.4 us (4%)
    reduce_sum x16, other arithmetic, fetch_block(): dist_sq = jnp.sum(offset * offset, axis=2)  21.1 us
    mul x8, other arithmetic, force_step(): live[:, :, None, None] * others[:, :, 3, None, :]  14.8 us
    all_gather x1, blocking collectives, on_device(): extended = lax.all_gather(rimmed, 'dev', axis=0, tiled=True)  14.7 us
    all_gather x1, blocking collectives, on_device(): weight_ext = lax.all_gather(weight_rim, 'dev', axis=0, tiled=True)  14 us
    mul x16, other arithmetic, fetch_block(): shift_blk[:, :, None, None, None] * unit_first[None, None, :, None, None]  11.7 us
    convert_element_type x16, other arithmetic, fetch_block(): ((block_at * NBLK + slot_range)[None, :] < counts[:, None]).astype(jnp.fl...  11.7 us
    reduce_sum x8, other arithmetic, density_step(): jnp.sum(live[:, :, None, None] * others[:, :, 3, None, :] * kernel, axis=...  11.5 us
    reduce_sum x8, other arithmetic, force_step(): return total - jnp.sum(factor[:, :, None] * offset, axis=(1, 4))  11.1 us
  transfers between devices with their start and end apart: 4, of which 3 were waited for; matrix products, arithmetic and copies ran while one was open for 2% of the time, Pallas kernels for 0%

commit v1 on v0

v1 whole, which is shorter than its diff:
```python
import functools
import math

import jax
import jax.numpy as jnp
from jax import lax
from jax.experimental import pallas as pl
from jax.experimental.pallas import tpu as pltpu
from jax.sharding import Mesh
from jax.sharding import PartitionSpec as P

NORM = 21.0 / (16.0 * math.pi)
TINY = 1e-30
ROWS = 8
UNROLL = 4


def split3(v):
    hi = v.astype(jnp.bfloat16).astype(jnp.float32)
    rest = v - hi
    mid = rest.astype(jnp.bfloat16).astype(jnp.float32)
    return hi, mid, rest - mid


def right_parts(v):
    hi, mid, low = split3(v)
    return jnp.concatenate([hi, mid, hi, low, hi, mid], axis=0).astype(jnp.bfloat16)


def left_parts(v):
    hi, mid, low = split3(v)
    stacked = jnp.concatenate([hi, hi, mid, hi, low, mid], axis=0)
    return jnp.transpose(stacked).astype(jnp.bfloat16)


def sum_parts(v):
    hi, mid, low = split3(v)
    return jnp.concatenate([hi, mid, low, jnp.zeros_like(low)], axis=0).astype(jnp.bfloat16)


def left_rows(v):
    row = lax.broadcasted_iota(jnp.int32, v.shape, 0)
    out = jnp.where(row < 3, -2.0 * v, jnp.where(row == 3, v[4:5], jnp.where(row == 4, 1.0, 0.0)))
    return out


def right_rows(v, shift):
    row = lax.broadcasted_iota(jnp.int32, v.shape, 0)
    moved = jnp.where(row == 0, shift, jnp.where(row == 4, shift * (2.0 * v[0:1] + shift), 0.0))
    return jnp.where(row < 5, v, 0.0) + moved


def table_index(cell_id, place, sizes):
    groups, depth, cores, own = sizes
    group_cells = depth * cores * own
    group_at, z_at, core_at = place[0], place[1], place[2]
    side = lax.rem(lax.div(cell_id, group_cells) - group_at + 1 + groups, groups)
    within = lax.rem(cell_id, group_cells)
    member = lax.div(within, own)
    z = lax.rem(lax.div(member, cores) - z_at + depth, depth)
    core = lax.rem(lax.rem(member, cores) - core_at + cores, cores)
    return ((side * cores + core) * depth + z) * own + lax.rem(within, own)


def table_cells(refs, sizes, fn):
    _, depth, cores, own = sizes
    per_ref = depth * own
    for at, ref in enumerate(refs):
        shift = float(at // cores - 1)

        def step(i, carry, ref=ref, at=at, shift=shift):
            fn(at * per_ref + i, ref[i], shift)
            return carry

        lax.fori_loop(0, per_ref, step, 0, unroll=4)


def density_kernel(sizes, place, lists, counts, own_ref, entropy, *rest):
    refs, (density, weight, table, nu_rows) = rest[:-4], rest[-4:]

    def fill(at, v, shift):
        nu = v[7:8]
        table[at] = right_parts((nu * nu) * right_rows(v, shift))
        nu_rows[at] = jnp.broadcast_to(nu, v.shape)

    table_cells(refs, sizes, fill)
    own = sizes[3]
    width = own_ref.shape[2]
    for cell in range(own):
        v = own_ref[cell]
        smooth = v[6:7]
        left = left_parts((4.0 / (smooth * smooth)) * left_rows(v))

        def step(k, total, cell=cell, left=left):
            for pair in range(UNROLL // 2):
                slot = k * UNROLL + 2 * pair
                at = [table_index(lists[cell, slot + e], place, sizes) for e in range(2)]
                right = jnp.concatenate([table[at[0]], table[at[1]]], axis=1)
                nu = jnp.concatenate([nu_rows[at[0]][:1], nu_rows[at[1]][:1]], axis=1)
                sq = jnp.maximum(jnp.dot(left, right, preferred_element_type=jnp.float32), TINY)
                base = jnp.maximum(4.0 * nu - sq * lax.rsqrt(sq), 0.0)
                base2 = base * base
                term = (base2 * base2) * (5.0 * nu - base)
                total = total + term[:, :width] + term[:, width:]
            return total

        total = lax.fori_loop(
            0, lax.div(counts[cell], UNROLL), step, jnp.zeros((width, width), jnp.float32)
        )
        summed = jnp.sum(jnp.transpose(total), axis=0, keepdims=True)
        dens = (NORM / 256.0) / (smooth * smooth * smooth) * summed
        density[cell : cell + 1] = dens
        weight[cell : cell + 1] = entropy[cell : cell + 1] * jnp.exp(jnp.log(dens) * (-1.0 / 3.0))


def pair_sums(left, cell, place, sizes, lists, counts, table, sums, width):
    def step(k, total):
        for pair in range(UNROLL // 2):
            slot = k * UNROLL + 2 * pair
            at = [table_index(lists[cell, slot + e], place, sizes) for e in range(2)]
            right = jnp.concatenate([table[at[0]], table[at[1]]], axis=1)
            rows = jnp.concatenate([sums[at[0]], sums[at[1]]], axis=1)
            sq = jnp.maximum(jnp.dot(left, right, preferred_element_type=jnp.float32), TINY)
            base = jnp.maximum(1.0 - sq * lax.rsqrt(sq), 0.0)
            cube = base * base * base
            hi = cube.astype(jnp.bfloat16)
            low = (cube - hi.astype(jnp.float32)).astype(jnp.bfloat16)
            total = total + lax.dot_general(
                jnp.concatenate([hi, low], axis=1),
                jnp.concatenate([rows, rows], axis=1),
                (((1,), (1,)), ((), ())),
                preferred_element_type=jnp.float32,
            )
        return total

    total = lax.fori_loop(
        0, lax.div(counts[cell], UNROLL), step, jnp.zeros((width, 4 * ROWS), jnp.float32)
    )
    total = jnp.transpose(total)
    return total[:ROWS] + total[ROWS : 2 * ROWS] + total[2 * ROWS : 3 * ROWS]


def own_kernel(sizes, place, lists, counts, own_ref, *rest):
    refs, (out, table, sums) = rest[:-3], rest[-3:]

    def fill(at, v, shift):
        rows = right_rows(v, shift)
        table[at] = right_parts(rows)
        sums[at] = sum_parts(v[5:6] * rows)

    table_cells(refs, sizes, fill)
    for cell in range(sizes[3]):
        v = own_ref[cell]
        smooth = v[6:7]
        left = left_parts((0.25 / (smooth * smooth)) * left_rows(v))
        out[cell] = pair_sums(
            left, cell, place, sizes, lists, counts, table, sums, own_ref.shape[2]
        )


def other_kernel(sizes, place, lists, counts, own_ref, weight_own, part, weight_all, *rest):
    refs, (out, table, sums) = rest[:-3], rest[-3:]
    groups, depth, cores, own = sizes
    per_ref = depth * own

    def fill(at, v, shift):
        ref_at, in_ref = lax.div(at, per_ref), lax.rem(at, per_ref)
        side, core = lax.div(ref_at, cores), lax.rem(ref_at, cores)
        group = lax.rem(place[0] + side - 1 + groups, groups)
        z = lax.rem(place[1] + lax.div(in_ref, own), depth)
        source = (group * depth + z) * cores + lax.rem(place[2] + core, cores)
        weight = weight_all[source, pl.ds(lax.rem(in_ref, own), 1), :]
        rows = right_rows(v, shift)
        inv = 1.0 / v[6:7]
        inv2 = inv * inv
        table[at] = right_parts((0.25 * inv2) * rows)
        sums[at] = sum_parts((v[5:6] * weight * (inv2 * inv2 * inv)) * rows)

    table_cells(refs, sizes, fill)
    for cell in range(own):
        v = own_ref[cell]
        left = left_parts(left_rows(v))
        other = pair_sums(
            left, cell, place, sizes, lists, counts, table, sums, own_ref.shape[2]
        )
        inv = 1.0 / v[6:7]
        inv2 = inv * inv
        total = (weight_own[cell : cell + 1] * (inv2 * inv2 * inv)) * part[cell] + other
        for k in range(3):
            out[k, cell : cell + 1, :] = (5.0 * NORM) * (
                v[k : k + 1] * total[3:4] - total[k : k + 1]
            )


def call(kernel, name, out_shape, scratch, place, lists, counts, arrays):
    smem = pl.BlockSpec(memory_space=pltpu.SMEM)
    vmem = pl.BlockSpec(memory_space=pltpu.VMEM)
    many = isinstance(out_shape, tuple)
    return pl.pallas_call(
        kernel,
        name=name,
        out_shape=out_shape,
        in_specs=[smem] * 3 + [vmem] * len(arrays),
        out_specs=(vmem,) * len(out_shape) if many else vmem,
        scratch_shapes=scratch,
        cost_estimate=pl.CostEstimate(
            flops=4_000_000_000, bytes_accessed=4_000_000, transcendentals=4_000_000
        ),
    )(place, lists, counts, *arrays)


def on_device(particles, entropy, lists, counts):
    own, _, width = particles.shape
    groups, depth, cores = (lax.axis_size(a) for a in ("grp", "z", "core"))
    sizes = (groups, depth, cores, own)
    place = jnp.stack([lax.axis_index(a) for a in ("grp", "z", "core")]).astype(jnp.int32)

    coords = particles[:, :3] - 0.5
    mass, smooth = particles[:, 3:4], particles[:, 4:5]
    rows = jnp.concatenate(
        [
            coords,
            jnp.ones_like(mass),
            jnp.sum(coords * coords, axis=1, keepdims=True),
            mass,
            smooth,
            jnp.exp(jnp.log(mass) * 0.2),
        ],
        axis=1,
    )

    def shifted(block, axis, by):
        count = lax.axis_size(axis)
        return lax.ppermute(block, axis, [(i, (i - by) % count) for i in range(count)])

    order = [1, depth - 1] + list(range(2, depth - 1))
    got = {0: rows}
    for by in dict.fromkeys(b % depth for b in order):
        if by:
            got[by] = shifted(rows, "z", by)
    column = jnp.concatenate([got[by] for by in range(depth)], axis=0)
    sides = [shifted(column, "grp", -1), column, shifted(column, "grp", 1)]
    refs = []
    for side in sides:
        refs.append(side)
        for by in range(1, cores):
            refs.append(shifted(side, "core", by))

    cells = 3 * cores * depth * own
    shape = jax.ShapeDtypeStruct
    table = pltpu.VMEM((cells, 6 * ROWS, width), jnp.bfloat16)
    sums = pltpu.VMEM((cells, 4 * ROWS, width), jnp.bfloat16)
    density, weight = call(
        functools.partial(density_kernel, sizes),
        "density",
        (shape((own, width), jnp.float32), shape((own, width), jnp.float32)),
        [table, pltpu.VMEM((cells, ROWS, width), jnp.float32)],
        place,
        lists,
        counts,
        [rows, entropy, *refs],
    )
    everyone = groups * depth * cores
    weight_all = lax.all_to_all(
        jnp.broadcast_to(weight[None], (everyone, own, width)),
        ("grp", "z", "core"),
        0,
        0,
        tiled=True,
    )
    part = call(
        functools.partial(own_kernel, sizes),
        "own",
        shape((own, ROWS, width), jnp.float32),
        [table, sums],
        place,
        lists,
        counts,
        [rows, *refs],
    )
    accel = call(
        functools.partial(other_kernel, sizes),
        "other",
        shape((3, own, width), jnp.float32),
        [table, sums],
        place,
        lists,
        counts,
        [rows, weight, part, weight_all, *refs],
    )
    return density, jnp.transpose(accel, (1, 0, 2))


def solution(mesh):
    groups, members = mesh.devices.shape
    cores = 2 if members % 2 == 0 else 1
    split = Mesh(mesh.devices.reshape(groups, members // cores, cores), ("grp", "z", "core"))
    cells = ("grp", "z", "core")
    return jax.shard_map(
        on_device,
        mesh=split,
        in_specs=(P(cells, None, None), P(cells, None), P(cells, None), P(cells)),
        out_specs=(P(cells, None), P(cells, None, None)),
        check_vma=False,
    )
```

time: 149 us -> 111 us (0.74)
  the two profiles are of different devices: /device:TPU:0 before, /device:TPU:11 now
where the time goes in v1:
time: 111 us; the launch traced here: 113 us
  Pallas kernels  90.3 us (81%)
  starting transfers between devices  16.3 us (15%)
  local copies, waits for them, and re-layouts  4.32 us (4%)
  waiting for transfers between devices  1.18 us (1%)
    pallas_call x3, Pallas kernels, call(): pl.pallas_call(kernel, name=name, out_shape=out_shape, in_specs=[smem] *...  90.3 us
    ppermute x8, starting transfers between devices, shifted(): lax.ppermute(block, axis, [(i, (i - by) % count) for i in range(count)])  13.5 us
    all_to_all x1, starting transfers between devices, on_device(): lax.all_to_all(jnp.broadcast_to(weight[None], (everyone, own, width)), ('...  2.76 us
    unnamed x19, local copies, waits for them, and re-layouts  2.26 us
  transfers between devices with their start and end apart: 9, of which 2 were waited for; matrix products, arithmetic and copies ran while one was open for 1% of the time, Pallas kernels for 31%

profile of v1, /device:TPU:11, one launch (start us, length us, event | category | flops | bytes accessed | tf_op | source)
XLA Modules:
  0.0 113.3 jit_solution(8861520510641075457)
XLA Ops:
  0.6 0.0 copy-start.3
  0.7 0.7 copy-done.3
  1.3 0.1 slice-done
  1.4 0.7 slice-done.1
  2.1 0.2 collective-permute-start
  2.4 2.3 %collective-permute-start.1 = (f32[4,8,128]{2,1,0:T(8,128)S(1)}, f32[4,8,128]{2,1,0:T(8,128)S(1)}, u32[]{:S(2)}, u32[]{:S(2)}) collective-permute-start(f32[4,8,128]{2,1,0:T(8,128)S(1)} %concatenate.6.own_ref), channel_id=1, source_target_pairs={{0,4},{2,6},{4,0},{6,2},{1,5},{3,7},{5,1},{7,3},{8,12},{10,14},{12... | collective-permute-start | bytes 49160 | tf_op jit(solution)/shard_map/ppermute | solution.py:234
  4.7 2.2 %collective-permute-start.2 = (f32[4,8,128]{2,1,0:T(8,128)S(1)}, f32[4,8,128]{2,1,0:T(8,128)S(1)}, u32[]{:S(2)}, u32[]{:S(2)}) collective-permute-start(f32[4,8,128]{2,1,0:T(8,128)S(1)} %concatenate.6.own_ref), channel_id=1, source_target_pairs={{0,2},{2,4},{4,6},{6,0},{1,3},{3,5},{5,7},{7,1},{8,10},{10,12},{12... | collective-permute-start | bytes 49160 | tf_op jit(solution)/shard_map/ppermute | solution.py:234
  6.9 0.9 collective-permute-done.2
  7.7 1.3 %collective-permute-start.3 = (f32[16,8,128]{2,1,0:T(8,128)S(1)}, f32[16,8,128]{2,1,0:T(8,128)S(1)}, u32[]{:S(2)}, u32[]{:S(2)}) collective-permute-start(f32[16,8,128]{2,1,0:T(8,128)S(1)} %pad_maximum_fusion.rest_2_), channel_id=1, source_target_pairs={{0,8},{8,16},{16,24},{24,0},{1,9},{9,17},{17,25},{25,1},{2,10},{10... | collective-permute-start | bytes 196616 | tf_op jit(solution)/shard_map/ppermute | solution.py:234
  9.0 0.3 collective-permute-start.6
  9.3 2.6 %collective-permute-start.5 = (f32[16,8,128]{2,1,0:T(8,128)S(1)}, f32[16,8,128]{2,1,0:T(8,128)S(1)}, u32[]{:S(2)}, u32[]{:S(2)}) collective-permute-start(f32[16,8,128]{2,1,0:T(8,128)S(1)} %pad_maximum_fusion.rest_2_), channel_id=1, source_target_pairs={{0,1},{1,0},{2,3},{3,2},{4,5},{5,4},{6,7},{7,6},{8,9},{9,8},{10,11... | collective-permute-start | bytes 196616 | tf_op jit(solution)/shard_map/ppermute | solution.py:234
  11.9 2.2 %collective-permute-start.4 = (f32[16,8,128]{2,1,0:T(8,128)S(1)}, f32[16,8,128]{2,1,0:T(8,128)S(1)}, u32[]{:S(2)}, u32[]{:S(2)}) collective-permute-start(f32[16,8,128]{2,1,0:T(8,128)S(1)} %collective-permute-done.3.rest_0_), channel_id=1, source_target_pairs={{0,1},{1,0},{2,3},{3,2},{4,5},{5,4},{6,7},{7,6},{8,9},{9,8},{10,11... | collective-permute-start | bytes 196616 | tf_op jit(solution)/shard_map/ppermute | solution.py:234
  14.2 2.4 %collective-permute-start.7 = (f32[16,8,128]{2,1,0:T(8,128)S(1)}, f32[16,8,128]{2,1,0:T(8,128)S(1)}, u32[]{:S(2)}, u32[]{:S(2)}) collective-permute-start(f32[16,8,128]{2,1,0:T(8,128)S(1)} %collective-permute-done.6.rest_4_), channel_id=1, source_target_pairs={{0,1},{1,0},{2,3},{3,2},{4,5},{5,4},{6,7},{7,6},{8,9},{9,8},{10,11... | collective-permute-start | bytes 196616 | tf_op jit(solution)/shard_map/ppermute | solution.py:234
  16.5 0.6 pad_add_fusion.place
  17.1 0.3 collective-permute-done.7.rest_5_
  17.5 0.3 copy-done.6
  17.8 0.0 copy-done.7
  17.8 0.6 copy-done.8
  18.4 19.7 %density.1 = (f32[4,128]{1,0:T(4,128)}, f32[4,128]{1,0:T(4,128)}) custom-call(s32[3]{0:T(128)} %pad_add_fusion.place, s32[4,64]{1,0:T(4,128)} %lists.5, s32[4]{0:T(128)} %counts.5, f32[4,8,128]{2,1,0:T(8,128)} %copy-done.2, f32[4,128]{1,0:T(4,128)} %entropy.1, f32[16,8,128]{2,1,0:T(8,128)} %copy-done.4, f32[16,8,128]{2,1,0:T(8,128)} %copy-done.7, ...), custom_call_target="tpu_custom_call" | custom-call | flops 4000000000 | bytes 4000000 | tf_op jit(solution)/shard_map/density/pallas_call | solution.py:199
  38.1 1.3 %broadcast_in_dim.14 = f32[32,4,128]{2,1,0:T(4,128)} broadcast(f32[4,128]{1,0:T(4,128)} %get-tuple-element.5.weight_own), dimensions={1,2} | broadcast | bytes 67584 | tf_op jit(solution)/shard_map/broadcast_in_dim | solution.py:265
  39.4 2.8 %all-to-all-start = ((f32[32,4,128]{2,1,0:T(4,128)}), f32[32,4,128]{2,1,0:T(4,128)S(1)}, u32[]{:S(2)}, u32[]{:S(2)}) async-start(f32[32,4,128]{2,1,0:T(4,128)} %broadcast_in_dim.14), calls=%async_computation | async-start | bytes 131072 | tf_op jit(solution)/shard_map/all_to_all | solution.py:264
  42.2 34.6 %own.1.part = f32[4,8,128]{2,1,0:T(8,128)} custom-call(s32[3]{0:T(128)} %pad_add_fusion.place, s32[4,64]{1,0:T(4,128)} %lists.5, s32[4]{0:T(128)} %counts.5, f32[4,8,128]{2,1,0:T(8,128)} %copy-done.2, f32[16,8,128]{2,1,0:T(8,128)} %copy-done.4, f32[16,8,128]{2,1,0:T(8,128)} %copy-done.7, f32[16,8,128]{2,1,0:T(8,128)} %copy-done, f32[16,8,128]{2,1,0:T(8,128)} %copy-done.6, ...), custom_call_target="tpu_custom_call" | custom-call | flops 4000000000 | bytes 4000000 | tf_op jit(solution)/shard_map/own/pallas_call | solution.py:199
  76.8 0.6 copy-done.1
  77.4 35.9 %other.1 = f32[3,4,128]{2,1,0:T(4,128)} custom-call(s32[3]{0:T(128)} %pad_add_fusion.place, s32[4,64]{1,0:T(4,128)} %lists.5, s32[4]{0:T(128)} %counts.5, f32[4,8,128]{2,1,0:T(8,128)} %copy-done.2, f32[4,128]{1,0:T(4,128)} %get-tuple-element.5.weight_own, f32[4,8,128]{2,1,0:T(8,128)} %own.1.part, f32[32,4,128]{2,1,0:T(4,128)} %copy-done.1, ...), custom_call_target="tpu_custom_call" | custom-call | flops 4000000000 | bytes 4000000 | tf_op jit(solution)/shard_map/other/pallas_call | solution.py:199
  (27 shorter events, 0.1 us)
Async XLA Ops:
  0.6 0.7 copy-start.3
  0.6 0.8 slice-start
  1.4 0.7 slice-start.1
  2.1 5.6 %copy-start.2 = (f32[4,8,128]{2,1,0:T(8,128)}, f32[4,8,128]{2,1,0:T(8,128)S(1)}, u32[]{:S(2)}) copy-start(f32[4,8,128]{2,1,0:T(8,128)S(1)} %concatenate.6.own_ref) | copy-start | bytes 49156
  2.1 4.7 %collective-permute-start = (f32[4,8,128]{2,1,0:T(8,128)S(1)}, f32[4,8,128]{2,1,0:T(8,128)S(1)}, u32[]{:S(2)}, u32[]{:S(2)}) collective-permute-start(f32[4,8,128]{2,1,0:T(8,128)S(1)} %concatenate.6.own_ref), channel_id=1, source_target_pairs={{0,6},{2,0},{4,2},{6,4},{1,7},{3,1},{5,3},{7,5},{8,14},{10,8},{12,... | collective-permute-start | bytes 49160 | tf_op jit(solution)/shard_map/ppermute | solution.py:234
  2.4 4.5 %collective-permute-start.1 = (f32[4,8,128]{2,1,0:T(8,128)S(1)}, f32[4,8,128]{2,1,0:T(8,128)S(1)}, u32[]{:S(2)}, u32[]{:S(2)}) collective-permute-start(f32[4,8,128]{2,1,0:T(8,128)S(1)} %concatenate.6.own_ref), channel_id=1, source_target_pairs={{0,4},{2,6},{4,0},{6,2},{1,5},{3,7},{5,1},{7,3},{8,12},{10,14},{12... | collective-permute-start | bytes 49160 | tf_op jit(solution)/shard_map/ppermute | solution.py:234
  4.7 3.1 %collective-permute-start.2 = (f32[4,8,128]{2,1,0:T(8,128)S(1)}, f32[4,8,128]{2,1,0:T(8,128)S(1)}, u32[]{:S(2)}, u32[]{:S(2)}) collective-permute-start(f32[4,8,128]{2,1,0:T(8,128)S(1)} %concatenate.6.own_ref), channel_id=1, source_target_pairs={{0,2},{2,4},{4,6},{6,0},{1,3},{3,5},{5,7},{7,1},{8,10},{10,12},{12... | collective-permute-start | bytes 49160 | tf_op jit(solution)/shard_map/ppermute | solution.py:234
  7.7 9.7 %copy-start = (f32[16,8,128]{2,1,0:T(8,128)}, f32[16,8,128]{2,1,0:T(8,128)S(1)}, u32[]{:S(2)}) copy-start(f32[16,8,128]{2,1,0:T(8,128)S(1)} %pad_maximum_fusion.rest_2_) | copy-start | bytes 196612
  7.7 4.2 %collective-permute-start.3 = (f32[16,8,128]{2,1,0:T(8,128)S(1)}, f32[16,8,128]{2,1,0:T(8,128)S(1)}, u32[]{:S(2)}, u32[]{:S(2)}) collective-permute-start(f32[16,8,128]{2,1,0:T(8,128)S(1)} %pad_maximum_fusion.rest_2_), channel_id=1, source_target_pairs={{0,8},{8,16},{16,24},{24,0},{1,9},{9,17},{17,25},{25,1},{2,10},{10... | collective-permute-start | bytes 196616 | tf_op jit(solution)/shard_map/ppermute | solution.py:234
  9.0 5.1 %collective-permute-start.6 = (f32[16,8,128]{2,1,0:T(8,128)S(1)}, f32[16,8,128]{2,1,0:T(8,128)S(1)}, u32[]{:S(2)}, u32[]{:S(2)}) collective-permute-start(f32[16,8,128]{2,1,0:T(8,128)S(1)} %pad_maximum_fusion.rest_2_), channel_id=1, source_target_pairs={{0,24},{8,0},{16,8},{24,16},{1,25},{9,1},{17,9},{25,17},{2,26},{10... | collective-permute-start | bytes 196616 | tf_op jit(solution)/shard_map/ppermute | solution.py:234
  9.3 7.9 %collective-permute-start.5 = (f32[16,8,128]{2,1,0:T(8,128)S(1)}, f32[16,8,128]{2,1,0:T(8,128)S(1)}, u32[]{:S(2)}, u32[]{:S(2)}) collective-permute-start(f32[16,8,128]{2,1,0:T(8,128)S(1)} %pad_maximum_fusion.rest_2_), channel_id=1, source_target_pairs={{0,1},{1,0},{2,3},{3,2},{4,5},{5,4},{6,7},{7,6},{8,9},{9,8},{10,11... | collective-permute-start | bytes 196616 | tf_op jit(solution)/shard_map/ppermute | solution.py:234
  11.9 5.5 %copy-start.4 = (f32[16,8,128]{2,1,0:T(8,128)}, f32[16,8,128]{2,1,0:T(8,128)S(1)}, u32[]{:S(2)}) copy-start(f32[16,8,128]{2,1,0:T(8,128)S(1)} %collective-permute-done.3.rest_0_) | copy-start | bytes 196612
  11.9 5.2 %collective-permute-start.4 = (f32[16,8,128]{2,1,0:T(8,128)S(1)}, f32[16,8,128]{2,1,0:T(8,128)S(1)}, u32[]{:S(2)}, u32[]{:S(2)}) collective-permute-start(f32[16,8,128]{2,1,0:T(8,128)S(1)} %collective-permute-done.3.rest_0_), channel_id=1, source_target_pairs={{0,1},{1,0},{2,3},{3,2},{4,5},{5,4},{6,7},{7,6},{8,9},{9,8},{10,11... | collective-permute-start | bytes 196616 | tf_op jit(solution)/shard_map/ppermute | solution.py:234
  14.2 3.3 %copy-start.5 = (f32[16,8,128]{2,1,0:T(8,128)}, f32[16,8,128]{2,1,0:T(8,128)S(1)}, u32[]{:S(2)}) copy-start(f32[16,8,128]{2,1,0:T(8,128)S(1)} %collective-permute-done.6.rest_4_) | copy-start | bytes 196612
  14.2 3.3 %collective-permute-start.7 = (f32[16,8,128]{2,1,0:T(8,128)S(1)}, f32[16,8,128]{2,1,0:T(8,128)S(1)}, u32[]{:S(2)}, u32[]{:S(2)}) collective-permute-start(f32[16,8,128]{2,1,0:T(8,128)S(1)} %collective-permute-done.6.rest_4_), channel_id=1, source_target_pairs={{0,1},{1,0},{2,3},{3,2},{4,5},{5,4},{6,7},{7,6},{8,9},{9,8},{10,11... | collective-permute-start | bytes 196616 | tf_op jit(solution)/shard_map/ppermute | solution.py:234
  17.1 0.6 copy-start.6
  17.1 0.6 copy-start.7
  17.8 0.6 copy-start.8
  39.4 37.4 %all-to-all-start = ((f32[32,4,128]{2,1,0:T(4,128)}), f32[32,4,128]{2,1,0:T(4,128)S(1)}, u32[]{:S(2)}, u32[]{:S(2)}) async-start(f32[32,4,128]{2,1,0:T(4,128)} %broadcast_in_dim.14), calls=%async_computation | async-start | bytes 131072 | tf_op jit(solution)/shard_map/all_to_all | solution.py:264
  76.8 0.6 copy-start.1
